TPU v7x, 32 devices: a whole 2x2x4 slice. The times are simulated.
32 devices in a mesh: users: 8 (over y, x, core), hist: 4 (over z).
Axes of the slice: x: 2, y: 2, z: 4, core: 2. Of those that a mesh axis runs over, the one named last changes fastest.
Arguments:
- cand_x: bfloat16 [2048, 512], P(('users', 'hist')), parts along dimension 0, may hold values from -6 to 6
- hist_keys: bfloat16 [16384, 512], P(('users', 'hist')), parts along dimension 0, may hold values from -6 to 6
- hist_values: bfloat16 [16384, 512], P(('users', 'hist')), parts along dimension 0, may hold values from -6 to 6
- key_scale: bfloat16 [16384], P(('users', 'hist')), parts along dimension 0, may hold values from 0.5 to 2
- hist_len: int32 [8], P('users'), parts along dimension 0, may hold values from 512 to 2048
- cand_limit: int32 [2048], P('users'), parts along dimension 0, may hold values from 1 to 2048
- ln_gain: float32 [512], replicated, may hold values from 0.1 to 1.9
- w_qu: bfloat16 [512, 1024], replicated, may hold values from -0.25 to 0.25
- w_out: bfloat16 [512, 512], replicated, may hold values from -0.25 to 0.25
Outputs:
- scored: bfloat16 [2048, 512], P(('users', 'hist')), parts along dimension 0
There are 8 independent parts, one for each index of `users`. A program takes and returns all parts, laid end to end along the dimension named above; an argument that names none is the same for every part. Nothing has to cross between parts.
All inputs are finite; a program needn't handle non-finite values.
Results may differ from a plain program's by a relative error of at most 0.0058.
Values may be sent and summed in bfloat16 or wider, within the bound.
A program may use at most 64 MiB of HBM per device.

v0:
```python
import jax
import jax.numpy as jnp
from jax import lax
from jax.sharding import PartitionSpec as P

HEADS = 8


def from_behind(value, axis, steps):
    count = lax.axis_size(axis)
    pairs = [(source, (source + steps) % count) for source in range(count)]
    return lax.ppermute(value, axis, pairs)


def row_norm(values):
    center = jnp.mean(values, axis=-1, keepdims=True)
    spread = jnp.mean((values - center) ** 2, axis=-1, keepdims=True)
    return (values - center) / jnp.sqrt(spread + 1e-05)


def attend(query_rows, history_limits, key_rows, value_rows, scale_rows, offset_pos):
    count = query_rows.shape[0]
    length = key_rows.shape[0]
    width = query_rows.shape[1]
    head_size = width // HEADS
    query_head_blocks = query_rows.reshape(count, HEADS, head_size)
    key_head_blocks = key_rows.reshape(length, HEADS, head_size)
    value_head_blocks = value_rows.reshape(length, HEADS, head_size)
    attention_scores = jnp.einsum(
        "ufe,yfe->fuy", query_head_blocks, key_head_blocks, preferred_element_type=jnp.float32
    )
    factor = scale_rows.astype(jnp.float32) / jnp.sqrt(jnp.float32(head_size))
    attention_scores = attention_scores * factor[None, None, :]
    positions = offset_pos + jnp.arange(length, dtype=jnp.int32)
    visible = positions[None, :] < history_limits[:, None]
    weight_matrices = jnp.where(visible[None], jax.nn.silu(attention_scores), 0.0).astype(
        jnp.bfloat16
    )
    summed_output = jnp.einsum(
        "apn,naf->paf", weight_matrices, value_head_blocks, preferred_element_type=jnp.float32
    )
    return summed_output.reshape(count, width)


def on_device(
    cand_x, hist_keys, hist_values, key_scale, hist_len, cand_limit, ln_gain, w_qu, w_out
):
    own_rows = cand_x.shape[0]
    width = cand_x.shape[1]
    inputs32 = cand_x.astype(jnp.float32)
    normed = (row_norm(inputs32) * ln_gain).astype(jnp.bfloat16)
    projected = jax.nn.silu(jnp.dot(normed, w_qu, preferred_element_type=jnp.float32))
    query_vectors = projected[:, :width].astype(jnp.bfloat16)
    gating = projected[:, width:]
    all_limits = jnp.minimum(cand_limit, hist_len[0])
    my_index = lax.axis_index("hist")
    offset_pos = my_index * hist_keys.shape[0]
    members = lax.axis_size("hist")

    def turn(step, carry):
        moving, total = carry
        owner = (my_index - step.astype(jnp.int32) + members) % members
        limit_part = lax.dynamic_slice_in_dim(all_limits, owner * own_rows, own_rows, 0)
        total = total + attend(moving, limit_part, hist_keys, hist_values, key_scale, offset_pos)
        moving = from_behind(moving, "hist", 1)
        total = from_behind(total, "hist", 1)
        return (moving, total)

    empty = jnp.zeros((own_rows, width), jnp.float32)
    final_state = lax.fori_loop(0, members, turn, (query_vectors, empty))
    attended = final_state[1]
    mixed = (row_norm(attended) * gating).astype(jnp.bfloat16)
    return (inputs32 + jnp.dot(mixed, w_out, preferred_element_type=jnp.float32)).astype(
        jnp.bfloat16
    )


def solution(mesh):
    in_specs = (
        P(("users", "hist"), None),
        P(("users", "hist"), None),
        P(("users", "hist"), None),
        P(("users", "hist")),
        P("users"),
        P("users"),
        P(),
        P(),
        P(),
    )
    out_specs = P(("users", "hist"), None)
    return jax.shard_map(
        on_device, mesh=mesh, in_specs=in_specs, out_specs=out_specs, check_vma=False
    )
```

profile of v0, /device:TPU:0, one launch (start us, length us, event | category | flops | bytes accessed | tf_op | source)
XLA Modules:
  0.0 46.9 jit_solution(12077700227379645533)
XLA Ops:
  0.7 0.7 %broadcast_minimum_fusion = s32[256]{0:T(256)S(1)} fusion(s32[256]{0:T(256)} %param.16, s32[]{:T(128)} %bitcast.19), kind=kLoop, calls=%fused_computation.34 | loop fusion | flops 256 | bytes 2052 | tf_op jit(solution)/shard_map/min | solution.py:55
  1.4 0.9 %convert_reduce_fusion = f32[64]{0:T(128)S(1)} fusion(bf16[64,512]{1,0:T(8,128)(2,1)} %param.11), kind=kLoop, calls=%fused_computation.17 | loop fusion | flops 65472 | bytes 65792 | tf_op jit(solution)/shard_map/reduce_sum | solution.py:16
  2.4 0.2 fusion.11
  2.6 0.5 copy-done.8
  3.1 0.4 divide_multiply_fusion
  3.5 0.6 %copy-done.1 = bf16[512,512]{1,0:T(8,128)(2,1)S(1)} copy-done((bf16[512,512]{1,0:T(8,128)(2,1)S(1)}, bf16[512,512]{1,0:T(8,128)(2,1)}, u32[]{:S(2)}) %copy-start.1) | copy-done | bytes 524312
  4.1 0.2 copy.15
  4.4 0.8 %copy-done.2 = bf16[512,512]{1,0:T(8,128)(2,1)S(1)} copy-done((bf16[512,512]{1,0:T(8,128)(2,1)S(1)}, bf16[512,512]{1,0:T(8,128)(2,1)}, u32[]{:S(2)}) %copy-start.2) | copy-done | bytes 524312
  5.2 0.2 copy.16
  5.4 0.7 %copy-done.5 = bf16[512]{0:T(512)(128)(2,1)S(1)} copy-done((bf16[512]{0:T(512)(128)(2,1)S(1)}, bf16[512]{0:T(512)(128)(2,1)}, u32[]{:S(2)}) %copy-start.5) | copy-done | bytes 1048
  6.1 37.9 %while.17 = (s32[]{:T(128)}, bf16[64,512]{1,0:T(8,128)(2,1)S(1)}, f32[64,512]{1,0:T(8,128)S(1)}, s32[]{:T(128)}, s32[]{:T(128)}, /*index=5*/s32[256]{0:T(256)S(1...) while((s32[]{:T(128)}, bf16[64,512]{1,0:T(8,128)(2,1)S(1)}, ...), condition=%wide.region_3.4_spmd, body=%wide.region_2.3_spmd.sunk | while | flops 69010960 | bytes 3287192 | solution.py:70
  6.1 0.1 reshape.107
  6.4 0.6 %convolution_bitcast_fusion.2 = f32[64,8,64]{2,0,1:T(8,128)S(1)} fusion(bf16[512,8,64]{0,2,1:T(8,128)(2,1)S(1)} %bitcast.21, bf16[512,8,64]{0,2,1:T(8,128)(2,1)S(1)} %bitcast.20, f32[512]{0:T(512)S(1)} %convert_multiply_fusion.2, pred[64,512]{1,0:T(8,128)(4,1)S(1)} %broadcast_compare_fusion.2, bf16[64,8,64]{2,1,0:T(8,128)(2,1)S(1)} %reshape.107), kind=kOutput, calls=%fused_computation.1.clone.1 | convolution fusion | flops 68943872 | bytes 1280000 | tf_op jit(solution)/shard_map/while/body/eval_jaxpr/apn,naf->paf/dot_general | solution.py:39
  7.0 0.2 copy.23
  7.3 3.1 %collective-permute-start.1 = (f32[64,512]{1,0:T(8,128)S(1)}, f32[64,512]{1,0:T(8,128)S(1)}, u32[]{:S(2)}, u32[]{:S(2)}) collective-permute-start(f32[64,512]{1,0:T(8,128)S(1)} %add.144), channel_id=1, source_target_pairs={{0,1},{1,2},{2,3},{3,0},{4,5},{5,6},{6,7},{7,4},{8,9},{9,10},{10,1... | collective-permute-start | bytes 393224 | tf_op jit(solution)/shard_map/while/body/eval_jaxpr/ppermute | solution.py:12
  10.4 1.6 %collective-permute-start = (bf16[64,512]{1,0:T(8,128)(2,1)S(1)}, bf16[64,512]{1,0:T(8,128)(2,1)S(1)}, u32[]{:S(2)}, u32[]{:S(2)}) collective-permute-start(bf16[64,512]{1,0:T(8,128)(2,1)S(1)} %copy.28), channel_id=1, source_target_pairs={{0,1},{1,2},{2,3},{3,0},{4,5},{5,6},{6,7},{7,4},{8,9},{9,10},{10,1... | collective-permute-start | bytes 196616 | tf_op jit(solution)/shard_map/while/body/eval_jaxpr/ppermute | solution.py:12
  12.0 5.3 %collective-permute-done = bf16[64,512]{1,0:T(8,128)(2,1)S(1)} collective-permute-done((bf16[64,512]{1,0:T(8,128)(2,1)S(1)}, bf16[64,512]{1,0:T(8,128)(2,1)S(1)}, u32[]{:S(2)}, u32[]{:S(2)}) %collective-permute-start) | collective-permute-done | bytes 65568 | tf_op jit(solution)/shard_map/while/body/eval_jaxpr/ppermute | solution.py:12
  17.4 0.1 reshape.107
  17.7 0.6 %convolution_bitcast_fusion.2 = f32[64,8,64]{2,0,1:T(8,128)S(1)} fusion(bf16[512,8,64]{0,2,1:T(8,128)(2,1)S(1)} %bitcast.21, bf16[512,8,64]{0,2,1:T(8,128)(2,1)S(1)} %bitcast.20, f32[512]{0:T(512)S(1)} %convert_multiply_fusion.2, pred[64,512]{1,0:T(8,128)(4,1)S(1)} %broadcast_compare_fusion.2, bf16[64,8,64]{2,1,0:T(8,128)(2,1)S(1)} %reshape.107), kind=kOutput, calls=%fused_computation.1.clone.1 | convolution fusion | flops 68943872 | bytes 1280000 | tf_op jit(solution)/shard_map/while/body/eval_jaxpr/apn,naf->paf/dot_general | solution.py:39
  18.3 0.2 copy.23
  18.6 1.3 %collective-permute-start = (bf16[64,512]{1,0:T(8,128)(2,1)S(1)}, bf16[64,512]{1,0:T(8,128)(2,1)S(1)}, u32[]{:S(2)}, u32[]{:S(2)}) collective-permute-start(bf16[64,512]{1,0:T(8,128)(2,1)S(1)} %copy.28), channel_id=1, source_target_pairs={{0,1},{1,2},{2,3},{3,0},{4,5},{5,6},{6,7},{7,4},{8,9},{9,10},{10,1... | collective-permute-start | bytes 196616 | tf_op jit(solution)/shard_map/while/body/eval_jaxpr/ppermute | solution.py:12
  19.9 6.5 %collective-permute-done = bf16[64,512]{1,0:T(8,128)(2,1)S(1)} collective-permute-done((bf16[64,512]{1,0:T(8,128)(2,1)S(1)}, bf16[64,512]{1,0:T(8,128)(2,1)S(1)}, u32[]{:S(2)}, u32[]{:S(2)}) %collective-permute-start) | collective-permute-done | bytes 65568 | tf_op jit(solution)/shard_map/while/body/eval_jaxpr/ppermute | solution.py:12
  26.5 0.1 reshape.107
  26.8 0.6 %convolution_bitcast_fusion.2 = f32[64,8,64]{2,0,1:T(8,128)S(1)} fusion(bf16[512,8,64]{0,2,1:T(8,128)(2,1)S(1)} %bitcast.21, bf16[512,8,64]{0,2,1:T(8,128)(2,1)S(1)} %bitcast.20, f32[512]{0:T(512)S(1)} %convert_multiply_fusion.2, pred[64,512]{1,0:T(8,128)(4,1)S(1)} %broadcast_compare_fusion.2, bf16[64,8,64]{2,1,0:T(8,128)(2,1)S(1)} %reshape.107), kind=kOutput, calls=%fused_computation.1.clone.1 | convolution fusion | flops 68943872 | bytes 1280000 | tf_op jit(solution)/shard_map/while/body/eval_jaxpr/apn,naf->paf/dot_general | solution.py:39
  27.4 0.2 copy.23
  27.9 7.4 %collective-permute-done = bf16[64,512]{1,0:T(8,128)(2,1)S(1)} collective-permute-done((bf16[64,512]{1,0:T(8,128)(2,1)S(1)}, bf16[64,512]{1,0:T(8,128)(2,1)S(1)}, u32[]{:S(2)}, u32[]{:S(2)}) %collective-permute-start) | collective-permute-done | bytes 65568 | tf_op jit(solution)/shard_map/while/body/eval_jaxpr/ppermute | solution.py:12
  35.6 0.6 %convolution_bitcast_fusion.2 = f32[64,8,64]{2,0,1:T(8,128)S(1)} fusion(bf16[512,8,64]{0,2,1:T(8,128)(2,1)S(1)} %bitcast.21, bf16[512,8,64]{0,2,1:T(8,128)(2,1)S(1)} %bitcast.20, f32[512]{0:T(512)S(1)} %convert_multiply_fusion.2, pred[64,512]{1,0:T(8,128)(4,1)S(1)} %broadcast_compare_fusion.2, bf16[64,8,64]{2,1,0:T(8,128)(2,1)S(1)} %reshape.107), kind=kOutput, calls=%fused_computation.1.clone.1 | convolution fusion | flops 68943872 | bytes 1280000 | tf_op jit(solution)/shard_map/while/body/eval_jaxpr/apn,naf->paf/dot_general | solution.py:39
  36.2 0.2 copy.23
  36.6 7.4 %collective-permute-done = bf16[64,512]{1,0:T(8,128)(2,1)S(1)} collective-permute-done((bf16[64,512]{1,0:T(8,128)(2,1)S(1)}, bf16[64,512]{1,0:T(8,128)(2,1)S(1)}, u32[]{:S(2)}, u32[]{:S(2)}) %collective-permute-start) | collective-permute-done | bytes 65568 | tf_op jit(solution)/shard_map/while/body/eval_jaxpr/ppermute | solution.py:12
  44.1 0.2 multiply_reduce_fusion
  44.4 0.6 %copy-done.4 = bf16[64,512]{1,0:T(8,128)(2,1)S(1)} copy-done((bf16[64,512]{1,0:T(8,128)(2,1)S(1)}, bf16[64,512]{1,0:T(8,128)(2,1)}, u32[]{:S(2)}) %copy-start.4) | copy-done | bytes 65560
  45.0 1.9 %fusion.8 = bf16[64,512]{1,0:T(8,128)(2,1)} fusion(bf16[512,512]{1,0:T(8,128)(2,1)} %param.19, bf16[64,512]{1,0:T(8,128)(2,1)S(1)} %copy-done.4, f32[64,1024]{1,0:T(8,128)S(1)} %copy-done.7, f32[64,512]{1,0:T(8,128)S(1)} %get-tuple-element.226, f32[64]{0:T(128)S(1)} %add_sqrt_fusion, f32[64]{0:T(128)S(1)} %broadcast_multiply_fusion), kind=kOutput, calls=%fused_computation.14 | convolution fusion | flops 33783808 | bytes 918528 | tf_op jit(solution)/shard_map/dot_general | solution.py:73
  (58 shorter events, 1.9 us)
Async XLA Ops:
  0.0 2.6 %copy-start = (bf16[512,1024]{1,0:T(8,128)(2,1)S(1)}, bf16[512,1024]{1,0:T(8,128)(2,1)}, u32[]{:S(2)}) copy-start(bf16[512,1024]{1,0:T(8,128)(2,1)} %param.18) | copy-start | bytes 3145732
  0.0 2.4 %copy-start.3 = (bf16[64,512]{1,0:T(8,128)(2,1)S(1)}, bf16[64,512]{1,0:T(8,128)(2,1)}, u32[]{:S(2)}) copy-start(bf16[64,512]{1,0:T(8,128)(2,1)} %param.11) | copy-start | bytes 196612
  2.4 0.7 %copy-start.8 = (f32[512]{0:T(512)S(1)}, f32[512]{0:T(512)}, u32[]{:S(2)}) copy-start(f32[512]{0:T(512)} %param.17) | copy-start | bytes 6148
  3.1 1.0 %copy-start.1 = (bf16[512,512]{1,0:T(8,128)(2,1)S(1)}, bf16[512,512]{1,0:T(8,128)(2,1)}, u32[]{:S(2)}) copy-start(bf16[512,512]{1,0:T(8,128)(2,1)} %param.12) | copy-start | bytes 1572868
  3.5 0.9 %copy-start.6 = (f32[64,1024]{1,0:T(8,128)}, f32[64,1024]{1,0:T(8,128)S(1)}, u32[]{:S(2)}) copy-start(f32[64,1024]{1,0:T(8,128)S(1)} %divide_multiply_fusion) | copy-start | bytes 786436
  4.1 1.0 %copy-start.2 = (bf16[512,512]{1,0:T(8,128)(2,1)S(1)}, bf16[512,512]{1,0:T(8,128)(2,1)}, u32[]{:S(2)}) copy-start(bf16[512,512]{1,0:T(8,128)(2,1)} %param.13) | copy-start | bytes 1572868
  5.4 0.7 %copy-start.5 = (bf16[512]{0:T(512)(128)(2,1)S(1)}, bf16[512]{0:T(512)(128)(2,1)}, u32[]{:S(2)}) copy-start(bf16[512]{0:T(512)(128)(2,1)} %param.14) | copy-start | bytes 3076
  6.1 38.3 %copy-start.7 = (f32[64,1024]{1,0:T(8,128)S(1)}, f32[64,1024]{1,0:T(8,128)}, u32[]{:S(2)}) copy-start(f32[64,1024]{1,0:T(8,128)} %copy-done.6) | copy-start | bytes 786436
  7.3 10.0 %collective-permute-start.1 = (f32[64,512]{1,0:T(8,128)S(1)}, f32[64,512]{1,0:T(8,128)S(1)}, u32[]{:S(2)}, u32[]{:S(2)}) collective-permute-start(f32[64,512]{1,0:T(8,128)S(1)} %add.144), channel_id=1, source_target_pairs={{0,1},{1,2},{2,3},{3,0},{4,5},{5,6},{6,7},{7,4},{8,9},{9,10},{10,1... | collective-permute-start | bytes 393224 | tf_op jit(solution)/shard_map/while/body/eval_jaxpr/ppermute | solution.py:12
  10.4 6.9 %collective-permute-start = (bf16[64,512]{1,0:T(8,128)(2,1)S(1)}, bf16[64,512]{1,0:T(8,128)(2,1)S(1)}, u32[]{:S(2)}, u32[]{:S(2)}) collective-permute-start(bf16[64,512]{1,0:T(8,128)(2,1)S(1)} %copy.28), channel_id=1, source_target_pairs={{0,1},{1,2},{2,3},{3,0},{4,5},{5,6},{6,7},{7,4},{8,9},{9,10},{10,1... | collective-permute-start | bytes 196616 | tf_op jit(solution)/shard_map/while/body/eval_jaxpr/ppermute | solution.py:12
  18.6 7.9 %collective-permute-start.1 = (f32[64,512]{1,0:T(8,128)S(1)}, f32[64,512]{1,0:T(8,128)S(1)}, u32[]{:S(2)}, u32[]{:S(2)}) collective-permute-start(f32[64,512]{1,0:T(8,128)S(1)} %add.144), channel_id=1, source_target_pairs={{0,1},{1,2},{2,3},{3,0},{4,5},{5,6},{6,7},{7,4},{8,9},{9,10},{10,1... | collective-permute-start | bytes 393224 | tf_op jit(solution)/shard_map/while/body/eval_jaxpr/ppermute | solution.py:12
  18.6 7.8 %collective-permute-start = (bf16[64,512]{1,0:T(8,128)(2,1)S(1)}, bf16[64,512]{1,0:T(8,128)(2,1)S(1)}, u32[]{:S(2)}, u32[]{:S(2)}) collective-permute-start(bf16[64,512]{1,0:T(8,128)(2,1)S(1)} %copy.28), channel_id=1, source_target_pairs={{0,1},{1,2},{2,3},{3,0},{4,5},{5,6},{6,7},{7,4},{8,9},{9,10},{10,1... | collective-permute-start | bytes 196616 | tf_op jit(solution)/shard_map/while/body/eval_jaxpr/ppermute | solution.py:12
  27.7 7.5 %collective-permute-start.1 = (f32[64,512]{1,0:T(8,128)S(1)}, f32[64,512]{1,0:T(8,128)S(1)}, u32[]{:S(2)}, u32[]{:S(2)}) collective-permute-start(f32[64,512]{1,0:T(8,128)S(1)} %add.144), channel_id=1, source_target_pairs={{0,1},{1,2},{2,3},{3,0},{4,5},{5,6},{6,7},{7,4},{8,9},{9,10},{10,1... | collective-permute-start | bytes 393224 | tf_op jit(solution)/shard_map/while/body/eval_jaxpr/ppermute | solution.py:12
  27.8 7.5 %collective-permute-start = (bf16[64,512]{1,0:T(8,128)(2,1)S(1)}, bf16[64,512]{1,0:T(8,128)(2,1)S(1)}, u32[]{:S(2)}, u32[]{:S(2)}) collective-permute-start(bf16[64,512]{1,0:T(8,128)(2,1)S(1)} %copy.28), channel_id=1, source_target_pairs={{0,1},{1,2},{2,3},{3,0},{4,5},{5,6},{6,7},{7,4},{8,9},{9,10},{10,1... | collective-permute-start | bytes 196616 | tf_op jit(solution)/shard_map/while/body/eval_jaxpr/ppermute | solution.py:12
  36.5 7.5 %collective-permute-start.1 = (f32[64,512]{1,0:T(8,128)S(1)}, f32[64,512]{1,0:T(8,128)S(1)}, u32[]{:S(2)}, u32[]{:S(2)}) collective-permute-start(f32[64,512]{1,0:T(8,128)S(1)} %add.144), channel_id=1, source_target_pairs={{0,1},{1,2},{2,3},{3,0},{4,5},{5,6},{6,7},{7,4},{8,9},{9,10},{10,1... | collective-permute-start | bytes 393224 | tf_op jit(solution)/shard_map/while/body/eval_jaxpr/ppermute | solution.py:12
  36.6 7.5 %collective-permute-start = (bf16[64,512]{1,0:T(8,128)(2,1)S(1)}, bf16[64,512]{1,0:T(8,128)(2,1)S(1)}, u32[]{:S(2)}, u32[]{:S(2)}) collective-permute-start(bf16[64,512]{1,0:T(8,128)(2,1)S(1)} %copy.28), channel_id=1, source_target_pairs={{0,1},{1,2},{2,3},{3,0},{4,5},{5,6},{6,7},{7,4},{8,9},{9,10},{10,1... | collective-permute-start | bytes 196616 | tf_op jit(solution)/shard_map/while/body/eval_jaxpr/ppermute | solution.py:12
  44.1 0.8 %copy-start.4 = (bf16[64,512]{1,0:T(8,128)(2,1)S(1)}, bf16[64,512]{1,0:T(8,128)(2,1)}, u32[]{:S(2)}) copy-start(bf16[64,512]{1,0:T(8,128)(2,1)} %param.11) | copy-start | bytes 196612
where the time goes:
time: 47.3 us; the launch traced here: 46.9 us
  waiting for transfers between devices  26.7 us (56%)
  starting transfers between devices  6.27 us (13%)
  local copies, waits for them, and re-layouts  5.69 us (12%)
  matrix products  4.63 us (10%)
  other arithmetic  2.59 us (5%)
  between operations  0.87 us (2%)
    ppermute x8, waiting for transfers between devices, from_behind(): return lax.ppermute(value, axis, pairs)  26.7 us
    ppermute x8, starting transfers between devices, from_behind(): return lax.ppermute(value, axis, pairs)  6.27 us
    unnamed x18, local copies, waits for them, and re-layouts  3.22 us
    dot_general x4, matrix products, attend(): jnp.einsum('apn,naf->paf', weight_matrices, value_head_blocks, preferred_...  2.33 us
    dot_general x1, matrix products, on_device(): jnp.dot(mixed, w_out, preferred_element_type=jnp.float32)  1.93 us
    reduce_sum x2, other arithmetic, row_norm(): center = jnp.mean(values, axis=-1, keepdims=True)  1.06 us
  transfers between devices with their start and end apart: 8, of which 4 were waited for; matrix products, arithmetic and copies ran while one was open for 0% of the time, Pallas kernels for 0%

commit v1 on v0

v1 whole, which is shorter than its diff:
```python
import functools

import jax
import jax.numpy as jnp
from jax import lax
from jax.experimental import pallas as pl
from jax.experimental.pallas import tpu as pltpu
from jax.sharding import PartitionSpec as P

HEADS = 8
GROUP = 4
LANES = 128
MESH = pl.DeviceIdType.MESH


def partner_of(me, step, count):
    bit = 1
    partner = me
    while bit < count:
        if step & bit:
            partner = partner + bit * (1 - 2 * lax.rem(me // bit, 2))
        bit *= 2
    return partner


def half_silu(half):
    return half + half * jnp.tanh(half)


def row_norm(values):
    center = jnp.mean(values, axis=-1, keepdims=True)
    spread = jnp.mean((values - center) ** 2, axis=-1, keepdims=True)
    return (values - center) / jnp.sqrt(spread + 1e-05)


def kernel(
    count,
    x_hbm, keys_hbm, values_hbm, scale_hbm, len_hbm, limit_hbm, gain_hbm, wqu_hbm, wout_hbm,
    out_ref,
    x_buf, keys_buf, values_buf, scale_buf, len_buf, limit_buf, gain_buf, wqu_buf, wout_buf,
    keys_t, limit_col, got_x, send_sum, got_sum,
    local_sem, xs_sem, xr_sem, ss_sem, sr_sem,
):
    me = lax.axis_index("hist")
    rows, width = x_buf.shape
    length = keys_buf.shape[0]
    head = width // HEADS
    span = GROUP * head
    steps = sorted(range(1, count), key=lambda step: -step)

    barrier = pltpu.get_barrier_semaphore()
    for step in steps:
        pl.semaphore_signal(
            barrier, inc=1, device_id={"hist": partner_of(me, step, count)}, device_id_type=MESH
        )

    pairs = [
        (x_hbm, x_buf), (limit_hbm, limit_buf), (len_hbm, len_buf), (gain_hbm, gain_buf),
        (scale_hbm, scale_buf), (keys_hbm, keys_buf), (wqu_hbm, wqu_buf),
        (values_hbm, values_buf), (wout_hbm, wout_buf),
    ]
    loads = [
        pltpu.make_async_copy(src, dst, local_sem.at[i]) for i, (src, dst) in enumerate(pairs)
    ]
    for load in loads:
        load.start()
    x_in, limit_in, len_in, gain_in, scale_in, keys_in, wqu_in, values_in, wout_in = loads
    x_in.wait()
    limit_in.wait()
    len_in.wait()
    limits = jnp.minimum(limit_buf[...], len_buf[0]).astype(jnp.float32).reshape(1, -1)
    limit_col[...] = jnp.broadcast_to(limits, (LANES, limits.shape[1])).T

    pl.semaphore_wait(barrier, count - 1)
    x_copies = {}
    for step in steps:
        x_copies[step] = pltpu.make_async_remote_copy(
            src_ref=x_buf,
            dst_ref=got_x.at[step - 1],
            send_sem=xs_sem.at[step - 1],
            recv_sem=xr_sem.at[step - 1],
            device_id={"hist": partner_of(me, step, count)},
            device_id_type=MESH,
        )
        x_copies[step].start()

    gain_in.wait()
    scale_in.wait()
    keys_in.wait()
    keys_t[...] = keys_buf[...].T
    gain = gain_buf[...].reshape(1, width)
    factor_row = scale_buf[...].astype(jnp.float32).reshape(1, length) * (0.5 / head**0.5)
    positions = (
        lax.broadcasted_iota(jnp.int32, (rows, length), 1) + me * length
    ).astype(jnp.float32)
    head_of_lane = lax.broadcasted_iota(jnp.int32, (rows, span), 1) // head

    def normed_of(block):
        return (row_norm(block.astype(jnp.float32)) * gain).astype(jnp.bfloat16)

    def attend(normed, owner):
        raw = jnp.dot(normed, wqu_buf[:, :width], preferred_element_type=jnp.float32)
        queries = half_silu(raw * 0.5)
        own_limit = limit_col[pl.ds(pl.multiple_of(owner * rows, rows), rows), :]
        own_limit = jnp.concatenate([own_limit] * (length // LANES), axis=1)
        factor = jnp.where(positions < own_limit, factor_row, 0.0)
        factor = jnp.concatenate([factor] * GROUP, axis=0)
        parts = []
        for start in range(0, width, span):
            some = queries[:, start : start + span]
            stacked = jnp.concatenate(
                [jnp.where(head_of_lane == i, some, 0.0) for i in range(GROUP)], axis=0
            ).astype(jnp.bfloat16)
            scores = jnp.dot(
                stacked, keys_t[start : start + span, :], preferred_element_type=jnp.float32
            )
            weights = half_silu(scores * factor).astype(jnp.bfloat16)
            summed = jnp.dot(
                weights, values_buf[:, start : start + span], preferred_element_type=jnp.float32
            )
            part = summed[:rows]
            for i in range(1, GROUP):
                part = jnp.where(head_of_lane == i, summed[i * rows : (i + 1) * rows], part)
            parts.append(part)
        return jnp.concatenate(parts, axis=1)

    normed = normed_of(x_buf[...])
    wqu_in.wait()
    values_in.wait()
    total = attend(normed, me)
    gating = half_silu(
        0.5 * jnp.dot(normed, wqu_buf[:, width:], preferred_element_type=jnp.float32)
    )

    sum_copies = {}
    for step in steps:
        partner = partner_of(me, step, count)
        x_copies[step].wait_recv()
        send_sum[step - 1] = attend(normed_of(got_x[step - 1]), partner).astype(jnp.bfloat16)
        sum_copies[step] = pltpu.make_async_remote_copy(
            src_ref=send_sum.at[step - 1],
            dst_ref=got_sum.at[step - 1],
            send_sem=ss_sem.at[step - 1],
            recv_sem=sr_sem.at[step - 1],
            device_id={"hist": partner},
            device_id_type=MESH,
        )
        sum_copies[step].start()

    wout_in.wait()
    for step in steps:
        sum_copies[step].wait_recv()
        total = total + got_sum[step - 1].astype(jnp.float32)
    mixed = (row_norm(total) * gating).astype(jnp.bfloat16)
    scored = x_buf[...].astype(jnp.float32) + jnp.dot(
        mixed, wout_buf[...], preferred_element_type=jnp.float32
    )
    out_ref[...] = scored.astype(jnp.bfloat16)
    for step in steps:
        x_copies[step].wait_send()
        sum_copies[step].wait_send()


def on_device(*args):
    count = lax.axis_size("hist")
    cand_x, limit = args[0], args[5]
    rows, width = cand_x.shape
    length = args[1].shape[0]
    assert count & (count - 1) == 0
    peers = count - 1
    block = (peers, rows, width)
    scratch = [
        pltpu.SMEM(a.shape, a.dtype) if i == 4 else pltpu.VMEM(a.shape, a.dtype)
        for i, a in enumerate(args)
    ]
    scratch += [
        pltpu.VMEM((width, length), jnp.bfloat16),
        pltpu.VMEM((limit.shape[0], LANES), jnp.float32),
        pltpu.VMEM(block, jnp.bfloat16),
        pltpu.VMEM(block, jnp.bfloat16),
        pltpu.VMEM(block, jnp.bfloat16),
        pltpu.SemaphoreType.DMA((len(args),)),
    ]
    scratch += [pltpu.SemaphoreType.DMA((peers,))] * 4
    return pl.pallas_call(
        functools.partial(kernel, count),
        out_shape=jax.ShapeDtypeStruct((rows, width), jnp.bfloat16),
        in_specs=[pl.BlockSpec(memory_space=pl.ANY)] * len(args),
        out_specs=pl.BlockSpec(memory_space=pltpu.VMEM),
        scratch_shapes=scratch,
        compiler_params=pltpu.CompilerParams(
            collective_id=0, has_side_effects=True, vmem_limit_bytes=60 * 1024 * 1024
        ),
    )(*args)


def solution(mesh):
    both = ("users", "hist")
    in_specs = (
        P(both, None), P(both, None), P(both, None), P(both), P("users"), P("users"),
        P(), P(), P(),
    )
    return jax.shard_map(
        on_device, mesh=mesh, in_specs=in_specs, out_specs=P(both, None), check_vma=False
    )
```

time: 47.3 us -> 21.4 us (0.45)
  the two profiles are of different devices: /device:TPU:0 before, /device:TPU:10 now
where the time goes in v1:
time: 21.4 us; the launch traced here: 21.2 us
  Pallas kernels  19.1 us (89%)
  local copies, waits for them, and re-layouts  1.47 us (7%)
  between operations  0.66 us (3%)
    pallas_call x1, Pallas kernels, on_device(): pl.pallas_call(functools.partial(kernel, count), out_shape=jax.ShapeDtype...  19.1 us
    unnamed x1, local copies, waits for them, and re-layouts  1.47 us

profile of v1, /device:TPU:10, one launch (start us, length us, event | category | flops | bytes accessed | tf_op | source)
XLA Modules:
  0.0 21.2 jit_solution(3653246236278908540)
XLA Ops:
  0.7 19.1 %shard_map.91 = bf16[64,512]{1,0:T(8,128)(2,1)} custom-call(bf16[64,512]{1,0:T(8,128)(2,1)} %x_hbm.1, bf16[512,512]{1,0:T(8,128)(2,1)} %keys_hbm.1, bf16[512,512]{1,0:T(8,128)(2,1)} %values_hbm.1, bf16[512]{0:T(512)(128)(2,1)} %scale_hbm.1, s32[1]{0:T(128)S(6)} %copy.11.len_hbm, s32[256]{0:T(256)} %limit_hbm.1, f32[512]{0:T(512)} %gain_hbm.1, ...), custom_call_target="tpu_custom_call" | custom-call | tf_op jit(solution)/shard_map/pallas_call | solution.py:185
  19.8 1.5 %copy.12 = bf16[64,512]{1,0:T(8,128)(2,1)} copy(bf16[64,512]{1,0:T(8,128)(2,1)} %shard_map.91) | data formatting | bytes 131072

commit v2 on v1

--- a/solution.py
+++ b/solution.py
@@ -10,6 +10,7 @@
 HEADS = 8
 GROUP = 4
 LANES = 128
+PIECES = 2
 MESH = pl.DeviceIdType.MESH
 
 
@@ -46,13 +47,19 @@
     length = keys_buf.shape[0]
     head = width // HEADS
     span = GROUP * head
-    steps = sorted(range(1, count), key=lambda step: -step)
+    half = count // 2
+    near = range(1, half)
+
+    def to(step):
+        return {"hist": partner_of(me, step, count)}
+
+    def pieces(step):
+        size = rows if step in near else rows // PIECES
+        return [(i, pl.ds(i * size, size)) for i in range(rows // size)]
 
     barrier = pltpu.get_barrier_semaphore()
-    for step in steps:
-        pl.semaphore_signal(
-            barrier, inc=1, device_id={"hist": partner_of(me, step, count)}, device_id_type=MESH
-        )
+    for step in range(1, half + 1):
+        pl.semaphore_signal(barrier, inc=1, device_id=to(step), device_id_type=MESH)
 
     pairs = [
         (x_hbm, x_buf), (limit_hbm, limit_buf), (len_hbm, len_buf), (gain_hbm, gain_buf),
@@ -65,25 +72,38 @@
     for load in loads:
         load.start()
     x_in, limit_in, len_in, gain_in, scale_in, keys_in, wqu_in, values_in, wout_in = loads
+    pl.semaphore_wait(barrier, half)
+    sends = []
+
+    def send(source, target, send_sem, recv_sem, step):
+        copy = pltpu.make_async_remote_copy(
+            src_ref=source, dst_ref=target, send_sem=send_sem, recv_sem=recv_sem,
+            device_id=to(step), device_id_type=MESH,
+        )
+        copy.start()
+        sends.append(copy)
+
+    def send_x(source, step, i, part, hop):
+        send(source, got_x.at[step - 1, part], xs_sem.at[step - 1, i], xr_sem.at[step - 1, i], hop)
+
+    def wait_block(buffer, sem, step, i, part):
+        block = buffer.at[step - 1, part]
+        pltpu.make_async_remote_copy(
+            src_ref=block, dst_ref=block, send_sem=sem.at[step - 1, i],
+            recv_sem=sem.at[step - 1, i], device_id=to(step), device_id_type=MESH,
+        ).wait_recv()
+
+    for step in [half, *near]:
+        for i, part in pieces(step):
+            send_x(x_hbm.at[part], step, i, part, step)
+
     x_in.wait()
     limit_in.wait()
     len_in.wait()
-    limits = jnp.minimum(limit_buf[...], len_buf[0]).astype(jnp.float32).reshape(1, -1)
+    limits = jnp.minimum(
+        limit_buf[...].reshape(1, -1), len_buf[...].reshape(1, 1)
+    ).astype(jnp.float32)
     limit_col[...] = jnp.broadcast_to(limits, (LANES, limits.shape[1])).T
-
-    pl.semaphore_wait(barrier, count - 1)
-    x_copies = {}
-    for step in steps:
-        x_copies[step] = pltpu.make_async_remote_copy(
-            src_ref=x_buf,
-            dst_ref=got_x.at[step - 1],
-            send_sem=xs_sem.at[step - 1],
-            recv_sem=xr_sem.at[step - 1],
-            device_id={"hist": partner_of(me, step, count)},
-            device_id_type=MESH,
-        )
-        x_copies[step].start()
-
     gain_in.wait()
     scale_in.wait()
     keys_in.wait()
@@ -98,18 +118,20 @@
     def normed_of(block):
         return (row_norm(block.astype(jnp.float32)) * gain).astype(jnp.bfloat16)
 
-    def attend(normed, owner):
+    def attend(normed, first):
+        rows = normed.shape[0]
+        lane_head = head_of_lane[:rows]
         raw = jnp.dot(normed, wqu_buf[:, :width], preferred_element_type=jnp.float32)
         queries = half_silu(raw * 0.5)
-        own_limit = limit_col[pl.ds(pl.multiple_of(owner * rows, rows), rows), :]
+        own_limit = limit_col[pl.ds(pl.multiple_of(first, rows), rows), :]
         own_limit = jnp.concatenate([own_limit] * (length // LANES), axis=1)
-        factor = jnp.where(positions < own_limit, factor_row, 0.0)
+        factor = jnp.where(positions[:rows] < own_limit, factor_row, 0.0)
         factor = jnp.concatenate([factor] * GROUP, axis=0)
         parts = []
         for start in range(0, width, span):
             some = queries[:, start : start + span]
             stacked = jnp.concatenate(
-                [jnp.where(head_of_lane == i, some, 0.0) for i in range(GROUP)], axis=0
+                [jnp.where(lane_head == i, some, 0.0) for i in range(GROUP)], axis=0
             ).astype(jnp.bfloat16)
             scores = jnp.dot(
                 stacked, keys_t[start : start + span, :], preferred_element_type=jnp.float32
@@ -120,45 +142,55 @@
             )
             part = summed[:rows]
             for i in range(1, GROUP):
-                part = jnp.where(head_of_lane == i, summed[i * rows : (i + 1) * rows], part)
+                part = jnp.where(lane_head == i, summed[i * rows : (i + 1) * rows], part)
             parts.append(part)
         return jnp.concatenate(parts, axis=1)
 
     normed = normed_of(x_buf[...])
     wqu_in.wait()
     values_in.wait()
-    total = attend(normed, me)
+    total = attend(normed, me * rows)
     gating = half_silu(
         0.5 * jnp.dot(normed, wqu_buf[:, width:], preferred_element_type=jnp.float32)
     )
 
-    sum_copies = {}
-    for step in steps:
-        partner = partner_of(me, step, count)
-        x_copies[step].wait_recv()
-        send_sum[step - 1] = attend(normed_of(got_x[step - 1]), partner).astype(jnp.bfloat16)
-        sum_copies[step] = pltpu.make_async_remote_copy(
-            src_ref=send_sum.at[step - 1],
-            dst_ref=got_sum.at[step - 1],
-            send_sem=ss_sem.at[step - 1],
-            recv_sem=sr_sem.at[step - 1],
-            device_id={"hist": partner},
-            device_id_type=MESH,
+    def answer(step, i, part):
+        first = partner_of(me, step, count) * rows + part.start
+        send_sum[step - 1, part] = attend(normed_of(got_x[step - 1, part]), first).astype(
+            jnp.bfloat16
         )
-        sum_copies[step].start()
+        send(
+            send_sum.at[step - 1, part], got_sum.at[step - 1, part],
+            ss_sem.at[step - 1, i], sr_sem.at[step - 1, i], step,
+        )
+
+    for i, part in pieces(half):
+        wait_block(got_x, xr_sem, half, i, part)
+        for step in near:
+            send_x(got_x.at[half - 1, part], half + step, i, part, step)
+        answer(half, i, part)
+    for step in near:
+        for i, part in pieces(step):
+            wait_block(got_x, xr_sem, step, i, part)
+            answer(step, i, part)
+    for i in range(PIECES):
+        for step in range(half + 1, count):
+            part = pieces(step)[i][1]
+            wait_block(got_x, xr_sem, step, i, part)
+            answer(step, i, part)
 
     wout_in.wait()
-    for step in steps:
-        sum_copies[step].wait_recv()
+    for step in [*near, *range(half, count)]:
+        for i, part in pieces(step):
+            wait_block(got_sum, sr_sem, step, i, part)
         total = total + got_sum[step - 1].astype(jnp.float32)
     mixed = (row_norm(total) * gating).astype(jnp.bfloat16)
     scored = x_buf[...].astype(jnp.float32) + jnp.dot(
         mixed, wout_buf[...], preferred_element_type=jnp.float32
     )
     out_ref[...] = scored.astype(jnp.bfloat16)
-    for step in steps:
-        x_copies[step].wait_send()
-        sum_copies[step].wait_send()
+    for copy in sends:
+        copy.wait_send()
 
 
 def on_device(*args):
@@ -170,8 +202,7 @@
     peers = count - 1
     block = (peers, rows, width)
     scratch = [
-        pltpu.SMEM(a.shape, a.dtype) if i == 4 else pltpu.VMEM(a.shape, a.dtype)
-        for i, a in enumerate(args)
+        pltpu.VMEM(a.shape, a.dtype) for a in args
     ]
     scratch += [
         pltpu.VMEM((width, length), jnp.bfloat16),
@@ -181,7 +212,7 @@
         pltpu.VMEM(block, jnp.bfloat16),
         pltpu.SemaphoreType.DMA((len(args),)),
     ]
-    scratch += [pltpu.SemaphoreType.DMA((peers,))] * 4
+    scratch += [pltpu.SemaphoreType.DMA((peers, PIECES))] * 4
     return pl.pallas_call(
         functools.partial(kernel, count),
         out_shape=jax.ShapeDtypeStruct((rows, width), jnp.bfloat16),

time: 21.4 us -> 20.9 us (0.977)
  the two profiles are of different devices: /device:TPU:10 before, /device:TPU:0 now
where the time goes in v2:
time: 20.9 us; the launch traced here: 20.7 us
  Pallas kernels  18.6 us (89%)
  local copies, waits for them, and re-layouts  1.47 us (7%)
  between operations  0.66 us (3%)
    pallas_call x1, Pallas kernels, on_device(): pl.pallas_call(functools.partial(kernel, count), out_shape=jax.ShapeDtype...  18.6 us
    unnamed x1, local copies, waits for them, and re-layouts  1.47 us

profile of v2, /device:TPU:0, one launch (start us, length us, event | category | flops | bytes accessed | tf_op | source)
XLA Modules:
  0.0 20.7 jit_solution(7120021766734988308)
XLA Ops:
  0.7 18.6 %shard_map.91 = bf16[64,512]{1,0:T(8,128)(2,1)} custom-call(bf16[64,512]{1,0:T(8,128)(2,1)} %x_hbm.1, bf16[512,512]{1,0:T(8,128)(2,1)} %keys_hbm.1, bf16[512,512]{1,0:T(8,128)(2,1)} %values_hbm.1, bf16[512]{0:T(512)(128)(2,1)} %scale_hbm.1, s32[1]{0:T(128)S(6)} %copy.11.len_hbm, s32[256]{0:T(256)} %limit_hbm.1, f32[512]{0:T(512)} %gain_hbm.1, ...), custom_call_target="tpu_custom_call" | custom-call | tf_op jit(solution)/shard_map/pallas_call | solution.py:216
  19.2 1.5 %copy.12 = bf16[64,512]{1,0:T(8,128)(2,1)} copy(bf16[64,512]{1,0:T(8,128)(2,1)} %shard_map.91) | data formatting | bytes 131072
